TPU v7x, 32 devices: a whole 2x2x4 slice. The times are simulated.
32 devices in a mesh: batch: 4 (over y, x), proto: 8 (over z, core).
Axes of the slice: x: 2, y: 2, z: 4, core: 2. Of those that a mesh axis runs over, the one named last changes fastest.
Arguments:
- teacher_emb: bfloat16 [256, 2048], P('proto', 'batch'), may hold values from -22 to 22
- student_emb: bfloat16 [256, 2048], P('proto', 'batch'), may hold values from -6 to 6
- prototypes: bfloat16 [256, 65536], P('batch', 'proto'), may hold values from -16 to 16
Outputs:
- grad_proto: float32 [256, 65536], P('batch', 'proto')
- grad_student: float32 [256, 2048], P('proto', 'batch')
- loss: float32 [], replicated
All inputs are finite; a program needn't handle non-finite values.
Results may differ from a plain program's by a relative error of at most 0.00055.
The roundings to bfloat16 on the way count: a program that leaves them out, or rounds other values in their place, can miss the bound.
Values may be sent and summed in bfloat16 or wider, within the bound.
No kernel may reach another device: no remote copies, remote signals or barrier semaphores. Data moves between devices by JAX's collectives and lax.ppermute only.
A program may use at most 128 MiB of HBM per device.

v0:
```python
import jax
import jax.numpy as jnp
from jax import lax
from jax.sharding import PartitionSpec as P

ITERS = 3
teacher_temp = 0.07
student_temp = 0.1
epsilon = 1e-06


def unit(matrix):
    values = matrix.astype(jnp.float32)
    factor = lax.rsqrt(jnp.sum(values * values, axis=0, keepdims=True) + epsilon)
    return ((values * factor).astype(jnp.bfloat16), factor)


def cosine(left, right):
    return lax.dot_general(
        left, right, (((0,), (0,)), ((), ())), preferred_element_type=jnp.float32
    )


def shards(teacher_emb, student_emb, prototypes):
    teacher_full, student_full = (
        lax.all_gather(teacher_emb, "proto", axis=0, tiled=True),
        lax.all_gather(student_emb, "proto", axis=0, tiled=True),
    )
    proto_full = lax.all_gather(prototypes, "batch", axis=0, tiled=True)
    proto_unit, proto_scale = unit(proto_full)
    teacher_unit, unused = unit(teacher_full)
    student_unit, student_scale = unit(student_full)
    width = proto_full.shape[0]
    local_rows = teacher_full.shape[1]
    total_rows = local_rows * lax.axis_size("batch")
    expo = jnp.exp(cosine(teacher_unit, proto_unit) / teacher_temp)
    targets = expo
    for iteration in range(ITERS):
        column_total = lax.psum(jnp.sum(targets, axis=0), "batch")
        targets = targets / column_total[None, :]
        row_total = lax.psum(jnp.sum(targets, axis=1), "proto")
        targets = targets / row_total[:, None]
    cos_student = cosine(student_unit, proto_unit)
    logits = cos_student / student_temp
    partial_total = jnp.sum(jnp.exp(logits), axis=1)
    softmax_total = lax.psum(partial_total, "proto")
    logp = logits - jnp.log(softmax_total)[:, None]
    loss_part = -jnp.sum(targets * logp)
    loss = lax.psum(loss_part, ("batch", "proto")) / total_rows
    grad_logit = ((jnp.exp(logp) - targets) / (total_rows * student_temp)).astype(jnp.bfloat16)
    proto_rows = width // lax.axis_size("batch")
    crop_rows = width // lax.axis_size("proto")
    proto_start = lax.axis_index("batch") * proto_rows
    crop_start = lax.axis_index("proto") * crop_rows
    proto_own = lax.dynamic_slice_in_dim(proto_unit, proto_start, proto_rows, 0).astype(jnp.float32)
    student_own = lax.dynamic_slice_in_dim(student_unit, crop_start, crop_rows, 0).astype(
        jnp.float32
    )
    rows = student_unit
    proto_part = lax.psum_scatter(
        jnp.dot(rows, grad_logit, preferred_element_type=jnp.float32),
        "batch",
        scatter_dimension=0,
        tiled=True,
    )
    rows = proto_unit
    crop_part = lax.psum_scatter(
        lax.dot_general(
            rows, grad_logit, (((1,), (1,)), ((), ())), preferred_element_type=jnp.float32
        ),
        "proto",
        scatter_dimension=0,
        tiled=True,
    )
    proto_dot = lax.psum(jnp.sum(proto_own * proto_part, axis=0), "batch")
    crop_dot = lax.psum(jnp.sum(student_own * crop_part, axis=0), "proto")
    grad_proto = (proto_part - proto_own * proto_dot[None, :]) * proto_scale
    grad_student = (crop_part - student_own * crop_dot[None, :]) * student_scale
    return (grad_proto, grad_student, loss)


def solution(mesh):
    in_specs = (P("proto", "batch"), P("proto", "batch"), P("batch", "proto"))
    out_specs = (P("batch", "proto"), P("proto", "batch"), P())
    return jax.shard_map(shards, mesh=mesh, in_specs=in_specs, out_specs=out_specs, check_vma=False)
```

profile of v0, /device:TPU:0, one launch (start us, length us, event | category | flops | bytes accessed | tf_op | source)
XLA Modules:
  0.0 381.8 jit_solution(16406410473220215280)
XLA Ops:
  7.2 0.0 all-gather.2.cloned.1.call-start
  7.2 0.7 all-gather.2.cloned.1.call-update
  7.9 0.0 reduce-scatter.5.cloned.1.call-start
  7.9 16.1 %all_gather.11 = bf16[256,512]{1,0:T(8,128)(2,1)S(1)} all-gather(bf16[32,512]{1,0:T(8,128)(2,1)} %param.3), channel_id=1, replica_groups=mesh['batch'=4,'proto'=8] {'proto'}, dimensions={0}, use_global_device_ids=true | all-gather | bytes 294912 | tf_op jit(solution)/shard_map/all_gather | solution.py:26
  24.1 14.4 %all_gather.9 = bf16[256,512]{1,0:T(8,128)(2,1)S(1)} all-gather(bf16[32,512]{1,0:T(8,128)(2,1)} %param.4), channel_id=1, replica_groups=mesh['batch'=4,'proto'=8] {'proto'}, dimensions={0}, use_global_device_ids=true | all-gather | bytes 294912 | tf_op jit(solution)/shard_map/all_gather | solution.py:27
  38.5 0.1 fusion.18
  38.5 0.1 fusion.16
  38.7 26.5 %all-gather.2.cloned.1.call-done = bf16[256,8192]{1,0:T(8,128)(2,1)} async-done(((bf16[64,8192]{1,0:T(8,128)(2,1)}), bf16[256,8192]{1,0:T(8,128)(2,1)}) %all-gather.2.cloned.1.call-update) | async-done | bytes 4194320 | tf_op jit(solution)/shard_map/all_gather | solution.py:29
  65.1 3.1 fusion.11
  68.2 3.3 fusion.12
  71.6 0.0 copy-start
  71.6 2.0 copy-done
  73.6 7.2 %fusion.25 = (f32[8192]{0:T(1024)S(1)}, f32[512,8192]{1,0:T(8,128)}) fusion(bf16[256,8192]{1,0:T(8,128)(2,1)S(1)} %fusion.12, bf16[256,512]{1,0:T(8,128)(2,1)S(1)} %all_gather.11, f32[512]{0:T(512)S(1)} %add_rsqrt_fusion.1), kind=kOutput, calls=%fused_computation.44 | convolution fusion | flops 2156257280 | bytes 21268480 | tf_op jit(solution)/shard_map/dot_general | solution.py:19
  80.9 15.4 %psum.71 = f32[8192]{0:T(1024)S(1)} all-reduce(f32[8192]{0:T(1024)S(1)} %get-tuple-element.9), channel_id=1, replica_groups=mesh['batch'=4,'proto'=8] {'batch'}, use_global_device_ids=true, to_apply=%region_6.0 | all-reduce | flops 8192 | bytes 65536 | tf_op jit(solution)/shard_map/psum | solution.py:39
  96.3 7.0 %divide_reduce_fusion = f32[512]{0:T(512)S(1)} fusion(f32[512,8192]{1,0:T(8,128)} %get-tuple-element.10, f32[8192]{0:T(1024)S(1)} %psum.71), kind=kLoop, calls=%fused_computation.13 | loop fusion | flops 8388096 | bytes 16812032 | tf_op jit(solution)/shard_map/reduce_sum | solution.py:41
  103.3 13.6 %psum.72 = f32[512]{0:T(512)S(1)} all-reduce(f32[512]{0:T(512)S(1)} %divide_reduce_fusion), channel_id=1, replica_groups=mesh['batch'=4,'proto'=8] {'proto'}, use_global_device_ids=true, to_apply=%region_8.0 | all-reduce | flops 512 | bytes 4096 | tf_op jit(solution)/shard_map/psum | solution.py:41
  116.9 8.4 %fusion.7 = f32[8192]{0:T(1024)S(1)} fusion(f32[512,8192]{1,0:T(8,128)} %get-tuple-element.10, f32[512]{0:T(512)S(1)} %psum.72, f32[8192]{0:T(1024)S(1)} %psum.71), kind=kLoop, calls=%fused_computation.14 | loop fusion | flops 12574720 | bytes 16844800 | tf_op jit(solution)/shard_map/reduce_sum | solution.py:39
  125.3 15.1 %psum.73 = f32[8192]{0:T(1024)S(1)} all-reduce(f32[8192]{0:T(1024)S(1)} %fusion.7), channel_id=1, replica_groups=mesh['batch'=4,'proto'=8] {'batch'}, use_global_device_ids=true, to_apply=%region_10.0 | all-reduce | flops 8192 | bytes 65536 | tf_op jit(solution)/shard_map/psum | solution.py:39
  140.4 8.7 %fusion.8 = f32[512]{0:T(512)S(1)} fusion(f32[512,8192]{1,0:T(8,128)} %get-tuple-element.10, f32[8192]{0:T(1024)S(1)} %psum.73, f32[512]{0:T(512)S(1)} %psum.72, f32[8192]{0:T(1024)S(1)} %psum.71), kind=kLoop, calls=%fused_computation.15 | loop fusion | flops 16776704 | bytes 16846848 | tf_op jit(solution)/shard_map/reduce_sum | solution.py:41
  149.1 13.6 %psum.74 = f32[512]{0:T(512)S(1)} all-reduce(f32[512]{0:T(512)S(1)} %fusion.8), channel_id=1, replica_groups=mesh['batch'=4,'proto'=8] {'proto'}, use_global_device_ids=true, to_apply=%region_12.0 | all-reduce | flops 512 | bytes 4096 | tf_op jit(solution)/shard_map/psum | solution.py:41
  162.7 7.8 %fusion.9 = f32[8192]{0:T(1024)S(1)} fusion(f32[512,8192]{1,0:T(8,128)} %get-tuple-element.10, f32[512]{0:T(512)S(1)} %psum.74, f32[8192]{0:T(1024)S(1)} %psum.73, f32[512]{0:T(512)S(1)} %psum.72, f32[8192]{0:T(1024)S(1)} %psum.71), kind=kLoop, calls=%fused_computation.16 | loop fusion | flops 20963328 | bytes 16879616 | tf_op jit(solution)/shard_map/reduce_sum | solution.py:39
  170.5 15.3 %psum.75 = f32[8192]{0:T(1024)S(1)} all-reduce(f32[8192]{0:T(1024)S(1)} %fusion.9), channel_id=1, replica_groups=mesh['batch'=4,'proto'=8] {'batch'}, use_global_device_ids=true, to_apply=%region_14.0 | all-reduce | flops 8192 | bytes 65536 | tf_op jit(solution)/shard_map/psum | solution.py:39
  185.8 0.0 copy-start.1
  185.9 8.4 %fusion.10 = f32[512]{0:T(512)S(1)} fusion(f32[512,8192]{1,0:T(8,128)} %get-tuple-element.10, f32[8192]{0:T(1024)S(1)} %psum.75, f32[512]{0:T(512)S(1)} %psum.74, f32[8192]{0:T(1024)S(1)} %psum.73, f32[512]{0:T(512)S(1)} %psum.72, f32[8192]{0:T(1024)S(1)} %psum.71), kind=kLoop, calls=%fused_computation.17 | loop fusion | flops 25165312 | bytes 16881664 | tf_op jit(solution)/shard_map/reduce_sum | solution.py:41
  194.3 0.0 copy-done.1
  194.3 7.2 %exponential_reduce_fusion = (f32[512]{0:T(512)S(1)}, f32[512,8192]{1,0:T(8,128)}) fusion(bf16[256,512]{1,0:T(8,128)(2,1)S(1)} %fusion.17, bf16[256,8192]{1,0:T(8,128)(2,1)S(1)} %copy-done.1), kind=kOutput, calls=%fused_computation.12 | convolution fusion | flops 2155871744 | bytes 21235712 | tf_op jit(solution)/shard_map/dot_general | solution.py:19
  201.5 13.8 %all-reduce = (f32[512]{0:T(512)S(1)}, f32[512]{0:T(512)S(1)}) all-reduce(f32[512]{0:T(512)S(1)} %get-tuple-element.7, f32[512]{0:T(512)S(1)} %fusion.10), channel_id=1, replica_groups=mesh['batch'=4,'proto'=8] {'proto'}, use_global_device_ids=true, to_apply=%region_3.0 | all-reduce | flops 1024 | bytes 8192 | tf_op jit(solution)/shard_map/psum | solution.py:46
  215.3 0.0 copy-start.2
  215.3 15.3 %multiply_reduce_fusion = (f32[]{:T(128)}, bf16[512,8192]{1,0:T(8,128)(2,1)S(1)}) fusion(f32[512,8192]{1,0:T(8,128)} %get-tuple-element.8, f32[512]{0:T(512)S(1)} %log.3, f32[512,8192]{1,0:T(8,128)} %get-tuple-element.10, f32[512]{0:T(512)S(1)} %get-tuple-element.4, f32[8192]{0:T(1024)S(1)} %psum.75, f32[512]{0:T(512)S(1)} %psum.74, f32[8192]{0:T(1024)S(1)} %psum.73, ...), kind=kLoop, calls=%fused_computation.9 | loop fusion | flops 54525952 | bytes 42049540 | tf_op jit(solution)/shard_map/reduce_sum | solution.py:48
  230.5 0.0 copy-start.3
  230.5 3.2 copy-done.3
  233.7 0.0 copy-done.2
  233.7 3.2 fusion.27
  236.9 0.0 reduce-scatter.5.cloned.1.call-update
  236.9 0.0 reduce-scatter.3.cloned.1.call-start
  237.0 9.0 %fusion.26 = f32[256,8192]{1,0:T(8,128)} fusion(bf16[256,512]{1,0:T(8,128)(2,1)S(1)} %fusion.17, bf16[512,8192]{1,0:T(8,128)(2,1)} %copy-done.3), kind=kOutput, calls=%fused_computation.45 | convolution fusion | flops 2147483648 | bytes 17039360 | tf_op jit(solution)/shard_map/dot_general | solution.py:61
  246.0 0.0 reduce-scatter.3.cloned.1.call-update
  246.7 37.5 %psum.79 = f32[]{:T(128)} all-reduce(f32[]{:T(128)S(6)} %neg.3), channel_id=1, replica_groups=mesh['batch'=4,'proto'=8] {'batch','proto'}, use_global_device_ids=true, to_apply=%region_24.0 | all-reduce | flops 1 | bytes 8 | tf_op jit(solution)/shard_map/psum | solution.py:49
  284.8 0.0 reduce-scatter.5.cloned.1.call-done
  284.9 0.9 fusion.22
  285.8 15.5 %psum.78 = f32[512]{0:T(512)S(1)} all-reduce(f32[512]{0:T(512)S(1)} %fusion.22), channel_id=1, replica_groups=mesh['batch'=4,'proto'=8] {'proto'}, use_global_device_ids=true, to_apply=%region_22.0 | all-reduce | flops 512 | bytes 4096 | tf_op jit(solution)/shard_map/psum | solution.py:76
  301.3 1.5 fusion.24
  302.7 50.4 %reduce-scatter.3.cloned.1.call-done = f32[64,8192]{1,0:T(8,128)} async-done(((f32[256,8192]{1,0:T(8,128)}), f32[64,8192]{1,0:T(8,128)}) %reduce-scatter.3.cloned.1.call-update) | async-done | bytes 2097168 | tf_op jit(solution)/shard_map/reduce_scatter | solution.py:60
  353.1 2.1 fusion.13
  355.2 15.4 %psum.77 = f32[8192]{0:T(1024)S(1)} all-reduce(f32[8192]{0:T(1024)S(1)} %fusion.13), channel_id=1, replica_groups=mesh['batch'=4,'proto'=8] {'batch'}, use_global_device_ids=true, to_apply=%region_19.0 | all-reduce | flops 8192 | bytes 65536 | tf_op jit(solution)/shard_map/psum | solution.py:75
  370.6 3.5 fusion.15
  (5 shorter events, 0.1 us)
Async XLA Ops:
  7.2 58.0 %all-gather.2.cloned.1.call-start = ((), (), s32[]{:S(2)}) async-start(), calls=%async_computation.2 | async-start | bytes 5242880 | tf_op jit(solution)/shard_map/all_gather | solution.py:29
  7.9 277.0 %reduce-scatter.5.cloned.1.call-start = ((), (), s32[]{:S(2)}) async-start(), calls=%async_computation.4 | async-start | bytes 589824 | tf_op jit(solution)/shard_map/reduce_scatter | solution.py:67
  71.6 2.0 copy-start
  185.8 8.4 %copy-start.1 = (bf16[256,8192]{1,0:T(8,128)(2,1)S(1)}, bf16[256,8192]{1,0:T(8,128)(2,1)}, u32[]{:S(2)}) copy-start(bf16[256,8192]{1,0:T(8,128)(2,1)} %copy-done) | copy-start | bytes 12582916
  215.3 18.5 %copy-start.2 = (bf16[256,8192]{1,0:T(8,128)(2,1)S(1)}, bf16[256,8192]{1,0:T(8,128)(2,1)}, u32[]{:S(2)}) copy-start(bf16[256,8192]{1,0:T(8,128)(2,1)} %copy-done) | copy-start | bytes 12582916
  230.5 3.2 copy-start.3
  236.9 116.2 %reduce-scatter.3.cloned.1.call-start = ((), (), s32[]{:S(2)}) async-start(), calls=%async_computation.3 | async-start | bytes 10485760 | tf_op jit(solution)/shard_map/reduce_scatter | solution.py:60
Sparse Core Ops, SparseCore 0:
  9.8 55.2 all-gather.1
  237.0 27.9 reduce-scatter.4
  268.1 84.9 reduce-scatter.2
where the time goes:
time: 382 us
  blocking collectives  186 us (49%)
  waiting for transfers between devices  77.5 us (20%)
  other arithmetic  70.2 us (18%)
  matrix products  26.6 us (7%)
  between operations  16.3 us (4%)
  local copies, waits for them, and re-layouts  5.26 us (1%)
    reduce_scatter x1, waiting for transfers between devices, shards(): lax.psum_scatter(jnp.dot(rows, grad_logit, preferred_element_type=jnp.flo...  50.4 us
    psum x3, blocking collectives, shards(): column_total = lax.psum(jnp.sum(targets, axis=0), 'batch')  45.8 us
    psum x1, blocking collectives, shards(): loss = lax.psum(loss_part, ('batch', 'proto')) / total_rows  37.5 us
    psum x2, blocking collectives, shards(): row_total = lax.psum(jnp.sum(targets, axis=1), 'proto')  27.2 us
    all_gather x1, waiting for transfers between devices, shards(): proto_full = lax.all_gather(prototypes, 'batch', axis=0, tiled=True)  26.5 us
    reduce_sum x3, other arithmetic, shards(): row_total = lax.psum(jnp.sum(targets, axis=1), 'proto')  24.2 us
    reduce_sum x2, other arithmetic, shards(): column_total = lax.psum(jnp.sum(targets, axis=0), 'batch')  16.2 us
    all_gather x1, blocking collectives, shards(): lax.all_gather(teacher_emb, 'proto', axis=0, tiled=True)  16.1 us
  transfers between devices with their start and end apart: 3, of which 2 were waited for; matrix products, arithmetic and copies ran while one was open for 3% of the time, Pallas kernels for 0%

commit v1 on v0

--- a/solution.py
+++ b/solution.py
@@ -36,7 +36,7 @@
     expo = jnp.exp(cosine(teacher_unit, proto_unit) / teacher_temp)
     targets = expo
     for iteration in range(ITERS):
-        column_total = lax.psum(jnp.sum(targets, axis=0), "batch")
+        column_total = jnp.sum(lax.all_gather(jnp.sum(targets, axis=0), "batch"), axis=0)
         targets = targets / column_total[None, :]
         row_total = lax.psum(jnp.sum(targets, axis=1), "proto")
         targets = targets / row_total[:, None]

time: 382 us -> 363 us (0.950)
  blocking collectives: 186 us -> 165 us
    psum x3 -> x0, blocking collectives: 45.8 us -> none  [shards(): column_total = lax.psum(jnp.sum(targets, axis=0), 'batch')]
    all_gather x0 -> x3, blocking collectives: none -> 24.6 us  [shards(): lax.all_gather(jnp.sum(targets, axis=0), 'batch')]
    reduce_sum x2 -> x5, other arithmetic: 16.2 us -> 16.4 us  [the longest x2 16.2 us: shards(): jnp.sum(targets, axis=0)]
where the time goes in v1:
time: 363 us; the launch traced here: 362 us
  blocking collectives  165 us (45%)
  waiting for transfers between devices  78.5 us (22%)
  other arithmetic  70.4 us (19%)
  matrix products  26.5 us (7%)
  between operations  16.3 us (4%)
  local copies, waits for them, and re-layouts  5.42 us (1%)
    reduce_scatter x1, waiting for transfers between devices, shards(): lax.psum_scatter(jnp.dot(rows, grad_logit, preferred_element_type=jnp.flo...  51.3 us
    psum x1, blocking collectives, shards(): loss = lax.psum(loss_part, ('batch', 'proto')) / total_rows  37.5 us
    psum x2, blocking collectives, shards(): row_total = lax.psum(jnp.sum(targets, axis=1), 'proto')  27.7 us
    all_gather x1, waiting for transfers between devices, shards(): proto_full = lax.all_gather(prototypes, 'batch', axis=0, tiled=True)  26.5 us
    all_gather x3, blocking collectives, shards(): lax.all_gather(jnp.sum(targets, axis=0), 'batch')  24.6 us
    reduce_sum x3, other arithmetic, shards(): row_total = lax.psum(jnp.sum(targets, axis=1), 'proto')  24.2 us
    reduce_sum x2, other arithmetic, shards(): jnp.sum(targets, axis=0)  16.2 us
    all_gather x1, blocking collectives, shards(): lax.all_gather(teacher_emb, 'proto', axis=0, tiled=True)  16.1 us
  transfers between devices with their start and end apart: 3, of which 2 were waited for; matrix products, arithmetic and copies ran while one was open for 3% of the time, Pallas kernels for 0%

profile of v1, /device:TPU:0, one launch (start us, length us, event | category | flops | bytes accessed | tf_op | source)
XLA Modules:
  0.0 362.3 jit_solution(291276691377635118)
XLA Ops:
  7.2 0.0 all-gather.5.cloned.1.call-start
  7.2 0.7 all-gather.5.cloned.1.call-update
  7.9 0.0 reduce-scatter.5.cloned.1.call-start
  7.9 16.1 %all_gather.29 = bf16[256,512]{1,0:T(8,128)(2,1)S(1)} all-gather(bf16[32,512]{1,0:T(8,128)(2,1)} %param.3), channel_id=1, replica_groups=mesh['batch'=4,'proto'=8] {'proto'}, dimensions={0}, use_global_device_ids=true | all-gather | bytes 294912 | tf_op jit(solution)/shard_map/all_gather | solution.py:26
  24.1 14.4 %all_gather.27 = bf16[256,512]{1,0:T(8,128)(2,1)S(1)} all-gather(bf16[32,512]{1,0:T(8,128)(2,1)} %param.4), channel_id=1, replica_groups=mesh['batch'=4,'proto'=8] {'proto'}, dimensions={0}, use_global_device_ids=true | all-gather | bytes 294912 | tf_op jit(solution)/shard_map/all_gather | solution.py:27
  38.5 0.1 fusion.18
  38.5 0.1 fusion.16
  38.7 26.5 %all-gather.5.cloned.1.call-done = bf16[256,8192]{1,0:T(8,128)(2,1)} async-done(((bf16[64,8192]{1,0:T(8,128)(2,1)}), bf16[256,8192]{1,0:T(8,128)(2,1)}) %all-gather.5.cloned.1.call-update) | async-done | bytes 4194320 | tf_op jit(solution)/shard_map/all_gather | solution.py:29
  65.1 3.1 fusion.11
  68.2 3.3 fusion.12
  71.6 0.0 copy-start
  71.6 2.0 copy-done
  73.6 7.2 %fusion.25 = (f32[8192]{0:T(1024)S(1)}, f32[512,8192]{1,0:T(8,128)}) fusion(bf16[256,8192]{1,0:T(8,128)(2,1)S(1)} %fusion.12, bf16[256,512]{1,0:T(8,128)(2,1)S(1)} %all_gather.29, f32[512]{0:T(512)S(1)} %add_rsqrt_fusion.1), kind=kOutput, calls=%fused_computation.44 | convolution fusion | flops 2156257280 | bytes 21268480 | tf_op jit(solution)/shard_map/dot_general | solution.py:19
  80.9 8.5 %all-gather = f32[32768]{0:T(1024)S(1)} all-gather(f32[8192]{0:T(1024)S(1)} %get-tuple-element.9), channel_id=2, replica_groups=mesh['batch'=4,'proto'=8] {'batch'}, dimensions={0}, use_global_device_ids=true | all-gather | bytes 163840 | tf_op jit(solution)/shard_map/all_gather | solution.py:39
  89.3 0.1 reshape.33
  89.4 0.1 reduce_sum.149
  89.5 7.0 %divide_reduce_fusion = f32[512]{0:T(512)S(1)} fusion(f32[512,8192]{1,0:T(8,128)} %get-tuple-element.10, f32[8192]{0:T(1024)S(1)} %reduce_sum.149), kind=kLoop, calls=%fused_computation.13 | loop fusion | flops 8388096 | bytes 16812032 | tf_op jit(solution)/shard_map/reduce_sum | solution.py:41
  96.5 14.1 %psum.50 = f32[512]{0:T(512)S(1)} all-reduce(f32[512]{0:T(512)S(1)} %divide_reduce_fusion), channel_id=1, replica_groups=mesh['batch'=4,'proto'=8] {'proto'}, use_global_device_ids=true, to_apply=%region_8.0 | all-reduce | flops 512 | bytes 4096 | tf_op jit(solution)/shard_map/psum | solution.py:41
  110.6 8.4 %fusion.7 = f32[8192]{0:T(1024)S(1)} fusion(f32[512,8192]{1,0:T(8,128)} %get-tuple-element.10, f32[512]{0:T(512)S(1)} %psum.50, f32[8192]{0:T(1024)S(1)} %reduce_sum.149), kind=kLoop, calls=%fused_computation.14 | loop fusion | flops 12574720 | bytes 16844800 | tf_op jit(solution)/shard_map/reduce_sum | solution.py:39
  119.0 7.8 %all-gather.1 = f32[32768]{0:T(1024)S(1)} all-gather(f32[8192]{0:T(1024)S(1)} %fusion.7), channel_id=3, replica_groups=mesh['batch'=4,'proto'=8] {'batch'}, dimensions={0}, use_global_device_ids=true | all-gather | bytes 163840 | tf_op jit(solution)/shard_map/all_gather | solution.py:39
  126.8 0.1 reshape.34
  126.9 0.1 reduce_sum.152
  127.0 8.7 %fusion.8 = f32[512]{0:T(512)S(1)} fusion(f32[512,8192]{1,0:T(8,128)} %get-tuple-element.10, f32[8192]{0:T(1024)S(1)} %reduce_sum.152, f32[512]{0:T(512)S(1)} %psum.50, f32[8192]{0:T(1024)S(1)} %reduce_sum.149), kind=kLoop, calls=%fused_computation.15 | loop fusion | flops 16776704 | bytes 16846848 | tf_op jit(solution)/shard_map/reduce_sum | solution.py:41
  135.7 13.6 %psum.51 = f32[512]{0:T(512)S(1)} all-reduce(f32[512]{0:T(512)S(1)} %fusion.8), channel_id=1, replica_groups=mesh['batch'=4,'proto'=8] {'proto'}, use_global_device_ids=true, to_apply=%region_12.0 | all-reduce | flops 512 | bytes 4096 | tf_op jit(solution)/shard_map/psum | solution.py:41
  149.3 7.8 %fusion.9 = f32[8192]{0:T(1024)S(1)} fusion(f32[512,8192]{1,0:T(8,128)} %get-tuple-element.10, f32[512]{0:T(512)S(1)} %psum.51, f32[8192]{0:T(1024)S(1)} %reduce_sum.152, f32[512]{0:T(512)S(1)} %psum.50, f32[8192]{0:T(1024)S(1)} %reduce_sum.149), kind=kLoop, calls=%fused_computation.16 | loop fusion | flops 20963328 | bytes 16879616 | tf_op jit(solution)/shard_map/reduce_sum | solution.py:39
  157.1 8.4 %all-gather.2 = f32[32768]{0:T(1024)S(1)} all-gather(f32[8192]{0:T(1024)S(1)} %fusion.9), channel_id=4, replica_groups=mesh['batch'=4,'proto'=8] {'batch'}, dimensions={0}, use_global_device_ids=true | all-gather | bytes 163840 | tf_op jit(solution)/shard_map/all_gather | solution.py:39
  165.4 0.1 reshape.35
  165.5 0.1 reduce_sum.155
  165.6 0.0 copy-start.1
  165.6 8.4 %fusion.10 = f32[512]{0:T(512)S(1)} fusion(f32[512,8192]{1,0:T(8,128)} %get-tuple-element.10, f32[8192]{0:T(1024)S(1)} %reduce_sum.155, f32[512]{0:T(512)S(1)} %psum.51, f32[8192]{0:T(1024)S(1)} %reduce_sum.152, f32[512]{0:T(512)S(1)} %psum.50, f32[8192]{0:T(1024)S(1)} %reduce_sum.149), kind=kLoop, calls=%fused_computation.17 | loop fusion | flops 25165312 | bytes 16881664 | tf_op jit(solution)/shard_map/reduce_sum | solution.py:41
  174.0 7.2 %exponential_reduce_fusion = (f32[512]{0:T(512)S(1)}, f32[512,8192]{1,0:T(8,128)}) fusion(bf16[256,512]{1,0:T(8,128)(2,1)S(1)} %fusion.17, bf16[256,8192]{1,0:T(8,128)(2,1)S(1)} %copy-done.1), kind=kOutput, calls=%fused_computation.12 | convolution fusion | flops 2155871744 | bytes 21235712 | tf_op jit(solution)/shard_map/dot_general | solution.py:19
  181.2 13.8 %all-reduce = (f32[512]{0:T(512)S(1)}, f32[512]{0:T(512)S(1)}) all-reduce(f32[512]{0:T(512)S(1)} %get-tuple-element.7, f32[512]{0:T(512)S(1)} %fusion.10), channel_id=1, replica_groups=mesh['batch'=4,'proto'=8] {'proto'}, use_global_device_ids=true, to_apply=%region_3.0 | all-reduce | flops 1024 | bytes 8192 | tf_op jit(solution)/shard_map/psum | solution.py:46
  195.0 15.3 %multiply_reduce_fusion = (f32[]{:T(128)}, bf16[512,8192]{1,0:T(8,128)(2,1)S(1)}) fusion(f32[512,8192]{1,0:T(8,128)} %get-tuple-element.8, f32[512]{0:T(512)S(1)} %log.3, f32[512,8192]{1,0:T(8,128)} %get-tuple-element.10, f32[512]{0:T(512)S(1)} %get-tuple-element.4, f32[8192]{0:T(1024)S(1)} %reduce_sum.155, f32[512]{0:T(512)S(1)} %psum.51, ...), kind=kLoop, calls=%fused_computation.9 | loop fusion | flops 54525952 | bytes 42049540 | tf_op jit(solution)/shard_map/reduce_sum | solution.py:48
  210.3 3.2 copy-done.3
  213.5 3.2 fusion.27
  216.6 0.0 reduce-scatter.5.cloned.1.call-update
  216.7 0.0 reduce-scatter.3.cloned.1.call-start
  216.7 9.0 %fusion.26 = f32[256,8192]{1,0:T(8,128)} fusion(bf16[256,512]{1,0:T(8,128)(2,1)S(1)} %fusion.17, bf16[512,8192]{1,0:T(8,128)(2,1)} %copy-done.3), kind=kOutput, calls=%fused_computation.45 | convolution fusion | flops 2147483648 | bytes 17039360 | tf_op jit(solution)/shard_map/dot_general | solution.py:61
  225.7 0.0 reduce-scatter.3.cloned.1.call-update
  226.3 37.5 %psum.55 = f32[]{:T(128)} all-reduce(f32[]{:T(128)S(6)} %neg.3), channel_id=1, replica_groups=mesh['batch'=4,'proto'=8] {'batch','proto'}, use_global_device_ids=true, to_apply=%region_24.0 | all-reduce | flops 1 | bytes 8 | tf_op jit(solution)/shard_map/psum | solution.py:49
  264.5 0.0 reduce-scatter.5.cloned.1.call-done
  264.6 0.9 fusion.22
  265.4 15.4 %psum.54 = f32[512]{0:T(512)S(1)} all-reduce(f32[512]{0:T(512)S(1)} %fusion.22), channel_id=1, replica_groups=mesh['batch'=4,'proto'=8] {'proto'}, use_global_device_ids=true, to_apply=%region_22.0 | all-reduce | flops 512 | bytes 4096 | tf_op jit(solution)/shard_map/psum | solution.py:76
  280.9 1.5 fusion.24
  282.3 51.3 %reduce-scatter.3.cloned.1.call-done = f32[64,8192]{1,0:T(8,128)} async-done(((f32[256,8192]{1,0:T(8,128)}), f32[64,8192]{1,0:T(8,128)}) %reduce-scatter.3.cloned.1.call-update) | async-done | bytes 2097168 | tf_op jit(solution)/shard_map/reduce_scatter | solution.py:60
  333.7 2.1 fusion.13
  335.8 15.4 %psum.53 = f32[8192]{0:T(1024)S(1)} all-reduce(f32[8192]{0:T(1024)S(1)} %fusion.13), channel_id=1, replica_groups=mesh['batch'=4,'proto'=8] {'batch'}, use_global_device_ids=true, to_apply=%region_19.0 | all-reduce | flops 8192 | bytes 65536 | tf_op jit(solution)/shard_map/psum | solution.py:75
  351.2 3.5 fusion.15
  (9 shorter events, 0.1 us)
Async XLA Ops:
  7.2 58.0 %all-gather.5.cloned.1.call-start = ((), (), s32[]{:S(2)}) async-start(), calls=%async_computation.2 | async-start | bytes 5242880 | tf_op jit(solution)/shard_map/all_gather | solution.py:29
  7.9 256.6 %reduce-scatter.5.cloned.1.call-start = ((), (), s32[]{:S(2)}) async-start(), calls=%async_computation.4 | async-start | bytes 589824 | tf_op jit(solution)/shard_map/reduce_scatter | solution.py:67
  71.6 2.0 copy-start
  165.6 8.4 %copy-start.1 = (bf16[256,8192]{1,0:T(8,128)(2,1)S(1)}, bf16[256,8192]{1,0:T(8,128)(2,1)}, u32[]{:S(2)}) copy-start(bf16[256,8192]{1,0:T(8,128)(2,1)} %copy-done) | copy-start | bytes 12582916
  195.0 18.5 %copy-start.2 = (bf16[256,8192]{1,0:T(8,128)(2,1)S(1)}, bf16[256,8192]{1,0:T(8,128)(2,1)}, u32[]{:S(2)}) copy-start(bf16[256,8192]{1,0:T(8,128)(2,1)} %copy-done) | copy-start | bytes 12582916
  210.3 3.2 copy-start.3
  216.7 117.0 %reduce-scatter.3.cloned.1.call-start = ((), (), s32[]{:S(2)}) async-start(), calls=%async_computation.3 | async-start | bytes 10485760 | tf_op jit(solution)/shard_map/reduce_scatter | solution.py:60
Sparse Core Ops, SparseCore 0:
  9.8 55.2 all-gather.4
  216.8 28.6 reduce-scatter.4
  248.6 85.0 reduce-scatter.2
